TPU v7x, 512 devices: a whole 4x8x8 slice. The times are simulated.
512 devices in a mesh: bulk: 32 (over x, y), valve: 16 (over z, core).
Axes of the slice: x: 4, y: 8, z: 8, core: 2. Of those that a mesh axis runs over, the one named last changes fastest.
Arguments:
- right_side: float32 [5, 256, 2048], P(None, 'bulk', 'valve'), may hold values from -0.005859375 to 0.005859375
- diag_inverse: float32 [5, 5, 256, 2048], P(None, None, 'bulk', 'valve'), as said below
- lower_jacobian: float32 [5, 5, 256, 2048], P(None, None, 'bulk', 'valve')
- upper_jacobian: float32 [5, 5, 256, 2048], P(None, None, 'bulk', 'valve')
- donor_index: int32 [32, 256, 8, 128], P('bulk', 'valve'), may hold values from 0 to 1023
- donor_weight: float32 [32, 256, 8, 128], P('bulk', 'valve'), may hold values from 0 to 0.25
- point_count: int32 [32, 256], P('bulk', 'valve'), may hold values from 32 to 128, as said below
- owner_device: int32 [32, 256], P('bulk', 'valve'), may hold values from 0 to 15, as said below
Outputs:
- update: float32 [5, 256, 2048], P(None, 'bulk', 'valve')
- fringe_rows: float32 [32, 1280, 5, 128], P('bulk', 'valve')
Inputs may be any that keep to these rules, and one draw needn't show every extreme that they name: `owner_device`: among the 16 blocks of one valve index at one bulk index, at most 5 name any one owner; in every draw one owner is named by exactly 5 blocks of every device. `point_count`: every device has a block with all 128 points live. `diag_inverse`: each cell's blocks are full, with nonzero entries off the diagonal.
All inputs are finite; a program needn't handle non-finite values.
Results may differ from a plain program's by a relative error of at most 0.00014.
Values sent between devices are 32-bit elements; how exact they have to be, the bound alone decides.
A program may use at most 64 MiB of HBM per device.

v0:
```python
import jax
import jax.numpy as jnp
from jax import lax
from jax.sharding import PartitionSpec as P

SWEEP_BLOCK = 8
POINTS = 128
CAPACITY = 5


PRECISE = lax.Precision.HIGHEST


def passed_along(value, axis, steps):
    count = lax.axis_size(axis)
    first, last = (max(0, -steps), min(count, count - steps))
    return lax.ppermute(value, axis, [(source, source + steps) for source in range(first, last)])


def apply_block(matrices, vectors):
    return jnp.sum(matrices * vectors[None, :, :], axis=1)


def compose_blocks(left, right):
    return jnp.sum(left[:, :, None, :] * right[None, :, :, :], axis=1)


def plane_sweep(diag_inverse, jacobian, source, incoming, downward, composite):
    planes = source.shape[1]
    plane_width = source.shape[2]

    def block_step(block_index, loop_carry):
        current, product, written = loop_carry
        start = planes - (block_index + 1) * SWEEP_BLOCK if downward else block_index * SWEEP_BLOCK
        results = [None] * SWEEP_BLOCK
        for offset in range(SWEEP_BLOCK):
            local_plane = SWEEP_BLOCK - 1 - offset if downward else offset
            inverse = diag_inverse[:, :, local_plane]
            jacobian_block = jacobian[:, :, local_plane]
            source_plane = source[:, local_plane]
            if downward:
                current = source_plane - apply_block(inverse, apply_block(jacobian_block, current))
            else:
                current = apply_block(inverse, source_plane - apply_block(jacobian_block, current))
            if composite:
                product = compose_blocks(-compose_blocks(inverse, jacobian_block), product)
            else:
                results[local_plane] = current
        if not composite:
            written = lax.dynamic_update_slice_in_dim(written, jnp.stack(results, axis=1), start, 1)
        return (current, product, written)

    identity_block = jnp.broadcast_to(
        jnp.eye(5, dtype=jnp.float32)[:, :, None], (5, 5, plane_width)
    )
    initial = (
        incoming,
        identity_block if composite else None,
        None if composite else jnp.zeros_like(source),
    )
    return lax.fori_loop(0, planes // SWEEP_BLOCK, block_step, initial)


def chain_input(product, offset, reverse):
    bulk_size = lax.axis_size("bulk")
    step_by = -1 if reverse else 1

    def relay(turn_index, loop_carry):
        arrived, leaving = loop_carry
        arrived = passed_along(leaving, "bulk", step_by)
        return (arrived, apply_block(product, arrived) + offset)

    arrived, _ = lax.fori_loop(0, bulk_size - 1, relay, (jnp.zeros_like(offset), offset))
    return arrived


def body(
    right_side,
    diag_inverse,
    lower_jacobian,
    upper_jacobian,
    donor_index,
    donor_weight,
    point_count,
    owner_device,
):
    plane_width = right_side.shape[2]
    zero_plane = jnp.zeros((5, plane_width), jnp.float32)
    lower_offset, lower_product, _ = plane_sweep(
        diag_inverse, lower_jacobian, right_side, zero_plane, False, True
    )
    lower_arrived = chain_input(lower_product, lower_offset, False)
    _, _, starred = plane_sweep(
        diag_inverse, lower_jacobian, right_side, lower_arrived, False, False
    )
    upper_offset, upper_product, _ = plane_sweep(
        diag_inverse, upper_jacobian, starred, zero_plane, True, True
    )
    upper_arrived = chain_input(upper_product, upper_offset, True)
    _, _, update = plane_sweep(diag_inverse, upper_jacobian, starred, upper_arrived, True, False)
    local_cells = update.reshape(5, -1)
    donor_cells = donor_index[0]
    picked = local_cells[:, donor_cells]
    values = jnp.sum(donor_weight[0][None] * picked, axis=2)
    live_mask = jnp.arange(POINTS)[None, :] < point_count[0][:, None]
    values = jnp.where(live_mask[None], values, jnp.float32(0.0))
    blocks = jnp.transpose(values, (1, 0, 2))
    row_count = blocks.shape[0]
    valve_size = lax.axis_size("valve")
    owner_row = owner_device[0]
    onehot = (owner_row[:, None] == jnp.arange(valve_size)[None, :]).astype(jnp.int32)
    before = jnp.cumsum(onehot, axis=0) - onehot
    slot_rank = jnp.sum(onehot * before, axis=1)
    slot_count = valve_size * CAPACITY
    destination = owner_row * CAPACITY + slot_rank
    placement = (jnp.arange(slot_count)[:, None] == destination[None, :]).astype(jnp.float32)
    outgoing = jnp.dot(placement, blocks.reshape(row_count, -1), precision=PRECISE).reshape(
        slot_count, 5, POINTS
    )
    received = lax.all_to_all(outgoing, "valve", split_axis=0, concat_axis=0, tiled=True)
    return (update, received[None])


def solution(mesh):
    in_specs = (
        P(None, "bulk", "valve"),
        P(None, None, "bulk", "valve"),
        P(None, None, "bulk", "valve"),
        P(None, None, "bulk", "valve"),
        P("bulk", "valve", None, None),
        P("bulk", "valve", None, None),
        P("bulk", "valve"),
        P("bulk", "valve"),
    )
    out_specs = (P(None, "bulk", "valve"), P("bulk", "valve", None, None))
    return jax.shard_map(body, mesh=mesh, in_specs=in_specs, out_specs=out_specs, check_vma=False)
```

profile of v0, /device:TPU:57, one launch (start us, length us, event | category | flops | bytes accessed | tf_op | source)
XLA Modules:
  0.0 607.1 jit_solution(4639897822346523980)
XLA Ops:
  8.6 215.1 %while.4 = (s32[]{:T(128)}, f32[5,128]{1,0:T(8,128)}, f32[5,128]{1,0:T(8,128)S(1)}, f32[5,5,128]{2,1,0:T(8,128)S(1)}, f32[5,128]{1,0:T(8,128)S(1)}, /*index=5*/s32[]{:T(128)}) while((s32[]{:T(128)}, f32[5,128]{1,0:T(8,128)}, f32[5,128]{1,0:T(8,128)S(1)}, f32[5,5,128]{2,1,0:T(8,128)S(1)}, f32[5,128]{1,0:T(8,128)S(1)}, ...), condition=%wide.region_34.35_spmd, body=%wide.region_32.34_spmd.sunk | while | flops 6402 | bytes 46217 | solution.py:73
  19.3 5.7 collective-permute-start
  26.3 5.7 collective-permute-start
  33.4 5.7 collective-permute-start
  40.4 5.7 collective-permute-start
  47.5 5.7 collective-permute-start
  54.5 5.8 collective-permute-start
  61.7 5.7 collective-permute-start
  68.7 5.7 collective-permute-start
  75.8 5.7 collective-permute-start
  82.8 5.7 collective-permute-start
  89.9 5.7 collective-permute-start
  96.9 5.7 collective-permute-start
  103.9 5.7 collective-permute-start
  111.0 5.7 collective-permute-start
  118.0 5.7 collective-permute-start
  125.1 5.7 collective-permute-start
  132.1 5.7 collective-permute-start
  139.2 5.7 collective-permute-start
  146.2 5.7 collective-permute-start
  153.2 5.7 collective-permute-start
  160.3 5.7 collective-permute-start
  167.4 5.7 collective-permute-start
  174.4 5.7 collective-permute-start
  181.4 5.7 collective-permute-start
  188.5 5.7 collective-permute-start
  195.5 5.7 collective-permute-start
  202.6 5.7 collective-permute-start
  209.6 5.7 collective-permute-start
  216.7 5.7 collective-permute-start
  226.1 218.7 %while.5 = (s32[]{:T(128)}, f32[5,128]{1,0:T(8,128)}, f32[5,128]{1,0:T(8,128)S(1)}, f32[5,5,128]{2,1,0:T(8,128)S(1)}, f32[5,128]{1,0:T(8,128)S(1)}, /*index=5*/s32[]{:T(128)}) while((s32[]{:T(128)}, f32[5,128]{1,0:T(8,128)}, f32[5,128]{1,0:T(8,128)S(1)}, f32[5,5,128]{2,1,0:T(8,128)S(1)}, f32[5,128]{1,0:T(8,128)S(1)}, ...), condition=%wide.region_85.86_spmd, body=%wide.region_83.85_spmd.sunk | while | flops 6402 | bytes 46217 | solution.py:73
  228.0 4.8 collective-permute-done.1
  242.3 4.5 collective-permute-done.1
  256.4 4.5 collective-permute-done.1
  270.5 4.5 collective-permute-done.1
  277.5 4.5 collective-permute-done.1
  291.6 4.5 collective-permute-done.1
  305.7 4.7 collective-permute-done.1
  312.9 4.5 collective-permute-done.1
  327.0 4.5 collective-permute-done.1
  341.0 4.5 collective-permute-done.1
  355.1 4.5 collective-permute-done.1
  362.2 4.5 collective-permute-done.1
  411.5 4.6 collective-permute-done.1
  450.1 54.4 %gather_fusion = f32[16384,5]{1,0:T(8,128)} fusion(f32[5,1024]{0,1:T(8,128)S(1)} %bitcast.276, s32[16384]{0:T(1024)S(1)} %fusion.1), kind=kCustom, calls=%fused_computation | custom fusion | bytes 720896 | tf_op jit(solution)/shard_map/gather | solution.py:103
  504.5 5.3 multiply_reduce_fusion.2
  511.6 81.7 %all-to-all-start = ((f32[80,5,128]{2,1,0:T(8,128)}), f32[80,5,128]{2,1,0:T(8,128)S(1)}, u32[]{:S(2)}, u32[]{:S(2)}) async-start(f32[80,5,128]{2,1,0:T(8,128)} %copy.120), calls=%async_computation | async-start | bytes 655360 | tf_op jit(solution)/shard_map/all_to_all | solution.py:120
  593.9 12.5 %all-to-all-done = f32[80,5,128]{2,1,0:T(8,128)S(1)} async-done(((f32[80,5,128]{2,1,0:T(8,128)}), f32[80,5,128]{2,1,0:T(8,128)S(1)}, u32[]{:S(2)}, u32[]{:S(2)}) %all-to-all-start) | async-done | bytes 204832 | tf_op jit(solution)/shard_map/all_to_all | solution.py:120
  (507 shorter events, 225.3 us)
Async XLA Ops:
  19.3 6.4 %collective-permute-start = (f32[5,128]{1,0:T(8,128)S(1)}, f32[5,128]{1,0:T(8,128)S(1)}, u32[]{:S(2)}, u32[]{:S(2)}) collective-permute-start(f32[5,128]{1,0:T(8,128)S(1)} %get-tuple-element.302), channel_id=1, source_target_pairs={{0,16},{16,32},{32,48},{48,64},{64,80},{80,96},{96,112},{112,128},... | collective-permute-start | bytes 7688 | tf_op jit(solution)/shard_map/while/body/eval_jaxpr/ppermute | solution.py:17
  26.3 6.4 %collective-permute-start = (f32[5,128]{1,0:T(8,128)S(1)}, f32[5,128]{1,0:T(8,128)S(1)}, u32[]{:S(2)}, u32[]{:S(2)}) collective-permute-start(f32[5,128]{1,0:T(8,128)S(1)} %get-tuple-element.302), channel_id=1, source_target_pairs={{0,16},{16,32},{32,48},{48,64},{64,80},{80,96},{96,112},{112,128},... | collective-permute-start | bytes 7688 | tf_op jit(solution)/shard_map/while/body/eval_jaxpr/ppermute | solution.py:17
  33.4 6.4 %collective-permute-start = (f32[5,128]{1,0:T(8,128)S(1)}, f32[5,128]{1,0:T(8,128)S(1)}, u32[]{:S(2)}, u32[]{:S(2)}) collective-permute-start(f32[5,128]{1,0:T(8,128)S(1)} %get-tuple-element.302), channel_id=1, source_target_pairs={{0,16},{16,32},{32,48},{48,64},{64,80},{80,96},{96,112},{112,128},... | collective-permute-start | bytes 7688 | tf_op jit(solution)/shard_map/while/body/eval_jaxpr/ppermute | solution.py:17
  40.4 6.4 %collective-permute-start = (f32[5,128]{1,0:T(8,128)S(1)}, f32[5,128]{1,0:T(8,128)S(1)}, u32[]{:S(2)}, u32[]{:S(2)}) collective-permute-start(f32[5,128]{1,0:T(8,128)S(1)} %get-tuple-element.302), channel_id=1, source_target_pairs={{0,16},{16,32},{32,48},{48,64},{64,80},{80,96},{96,112},{112,128},... | collective-permute-start | bytes 7688 | tf_op jit(solution)/shard_map/while/body/eval_jaxpr/ppermute | solution.py:17
  47.5 6.4 %collective-permute-start = (f32[5,128]{1,0:T(8,128)S(1)}, f32[5,128]{1,0:T(8,128)S(1)}, u32[]{:S(2)}, u32[]{:S(2)}) collective-permute-start(f32[5,128]{1,0:T(8,128)S(1)} %get-tuple-element.302), channel_id=1, source_target_pairs={{0,16},{16,32},{32,48},{48,64},{64,80},{80,96},{96,112},{112,128},... | collective-permute-start | bytes 7688 | tf_op jit(solution)/shard_map/while/body/eval_jaxpr/ppermute | solution.py:17
  54.5 6.6 %collective-permute-start = (f32[5,128]{1,0:T(8,128)S(1)}, f32[5,128]{1,0:T(8,128)S(1)}, u32[]{:S(2)}, u32[]{:S(2)}) collective-permute-start(f32[5,128]{1,0:T(8,128)S(1)} %get-tuple-element.302), channel_id=1, source_target_pairs={{0,16},{16,32},{32,48},{48,64},{64,80},{80,96},{96,112},{112,128},... | collective-permute-start | bytes 7688 | tf_op jit(solution)/shard_map/while/body/eval_jaxpr/ppermute | solution.py:17
  61.7 6.4 %collective-permute-start = (f32[5,128]{1,0:T(8,128)S(1)}, f32[5,128]{1,0:T(8,128)S(1)}, u32[]{:S(2)}, u32[]{:S(2)}) collective-permute-start(f32[5,128]{1,0:T(8,128)S(1)} %get-tuple-element.302), channel_id=1, source_target_pairs={{0,16},{16,32},{32,48},{48,64},{64,80},{80,96},{96,112},{112,128},... | collective-permute-start | bytes 7688 | tf_op jit(solution)/shard_map/while/body/eval_jaxpr/ppermute | solution.py:17
  68.7 6.4 %collective-permute-start = (f32[5,128]{1,0:T(8,128)S(1)}, f32[5,128]{1,0:T(8,128)S(1)}, u32[]{:S(2)}, u32[]{:S(2)}) collective-permute-start(f32[5,128]{1,0:T(8,128)S(1)} %get-tuple-element.302), channel_id=1, source_target_pairs={{0,16},{16,32},{32,48},{48,64},{64,80},{80,96},{96,112},{112,128},... | collective-permute-start | bytes 7688 | tf_op jit(solution)/shard_map/while/body/eval_jaxpr/ppermute | solution.py:17
  75.8 6.4 %collective-permute-start = (f32[5,128]{1,0:T(8,128)S(1)}, f32[5,128]{1,0:T(8,128)S(1)}, u32[]{:S(2)}, u32[]{:S(2)}) collective-permute-start(f32[5,128]{1,0:T(8,128)S(1)} %get-tuple-element.302), channel_id=1, source_target_pairs={{0,16},{16,32},{32,48},{48,64},{64,80},{80,96},{96,112},{112,128},... | collective-permute-start | bytes 7688 | tf_op jit(solution)/shard_map/while/body/eval_jaxpr/ppermute | solution.py:17
  82.8 6.4 %collective-permute-start = (f32[5,128]{1,0:T(8,128)S(1)}, f32[5,128]{1,0:T(8,128)S(1)}, u32[]{:S(2)}, u32[]{:S(2)}) collective-permute-start(f32[5,128]{1,0:T(8,128)S(1)} %get-tuple-element.302), channel_id=1, source_target_pairs={{0,16},{16,32},{32,48},{48,64},{64,80},{80,96},{96,112},{112,128},... | collective-permute-start | bytes 7688 | tf_op jit(solution)/shard_map/while/body/eval_jaxpr/ppermute | solution.py:17
  89.9 6.4 %collective-permute-start = (f32[5,128]{1,0:T(8,128)S(1)}, f32[5,128]{1,0:T(8,128)S(1)}, u32[]{:S(2)}, u32[]{:S(2)}) collective-permute-start(f32[5,128]{1,0:T(8,128)S(1)} %get-tuple-element.302), channel_id=1, source_target_pairs={{0,16},{16,32},{32,48},{48,64},{64,80},{80,96},{96,112},{112,128},... | collective-permute-start | bytes 7688 | tf_op jit(solution)/shard_map/while/body/eval_jaxpr/ppermute | solution.py:17
  96.9 6.4 %collective-permute-start = (f32[5,128]{1,0:T(8,128)S(1)}, f32[5,128]{1,0:T(8,128)S(1)}, u32[]{:S(2)}, u32[]{:S(2)}) collective-permute-start(f32[5,128]{1,0:T(8,128)S(1)} %get-tuple-element.302), channel_id=1, source_target_pairs={{0,16},{16,32},{32,48},{48,64},{64,80},{80,96},{96,112},{112,128},... | collective-permute-start | bytes 7688 | tf_op jit(solution)/shard_map/while/body/eval_jaxpr/ppermute | solution.py:17
  103.9 6.4 %collective-permute-start = (f32[5,128]{1,0:T(8,128)S(1)}, f32[5,128]{1,0:T(8,128)S(1)}, u32[]{:S(2)}, u32[]{:S(2)}) collective-permute-start(f32[5,128]{1,0:T(8,128)S(1)} %get-tuple-element.302), channel_id=1, source_target_pairs={{0,16},{16,32},{32,48},{48,64},{64,80},{80,96},{96,112},{112,128},... | collective-permute-start | bytes 7688 | tf_op jit(solution)/shard_map/while/body/eval_jaxpr/ppermute | solution.py:17
  111.0 6.4 %collective-permute-start = (f32[5,128]{1,0:T(8,128)S(1)}, f32[5,128]{1,0:T(8,128)S(1)}, u32[]{:S(2)}, u32[]{:S(2)}) collective-permute-start(f32[5,128]{1,0:T(8,128)S(1)} %get-tuple-element.302), channel_id=1, source_target_pairs={{0,16},{16,32},{32,48},{48,64},{64,80},{80,96},{96,112},{112,128},... | collective-permute-start | bytes 7688 | tf_op jit(solution)/shard_map/while/body/eval_jaxpr/ppermute | solution.py:17
  118.0 6.4 %collective-permute-start = (f32[5,128]{1,0:T(8,128)S(1)}, f32[5,128]{1,0:T(8,128)S(1)}, u32[]{:S(2)}, u32[]{:S(2)}) collective-permute-start(f32[5,128]{1,0:T(8,128)S(1)} %get-tuple-element.302), channel_id=1, source_target_pairs={{0,16},{16,32},{32,48},{48,64},{64,80},{80,96},{96,112},{112,128},... | collective-permute-start | bytes 7688 | tf_op jit(solution)/shard_map/while/body/eval_jaxpr/ppermute | solution.py:17
  125.1 6.4 %collective-permute-start = (f32[5,128]{1,0:T(8,128)S(1)}, f32[5,128]{1,0:T(8,128)S(1)}, u32[]{:S(2)}, u32[]{:S(2)}) collective-permute-start(f32[5,128]{1,0:T(8,128)S(1)} %get-tuple-element.302), channel_id=1, source_target_pairs={{0,16},{16,32},{32,48},{48,64},{64,80},{80,96},{96,112},{112,128},... | collective-permute-start | bytes 7688 | tf_op jit(solution)/shard_map/while/body/eval_jaxpr/ppermute | solution.py:17
  132.1 6.4 %collective-permute-start = (f32[5,128]{1,0:T(8,128)S(1)}, f32[5,128]{1,0:T(8,128)S(1)}, u32[]{:S(2)}, u32[]{:S(2)}) collective-permute-start(f32[5,128]{1,0:T(8,128)S(1)} %get-tuple-element.302), channel_id=1, source_target_pairs={{0,16},{16,32},{32,48},{48,64},{64,80},{80,96},{96,112},{112,128},... | collective-permute-start | bytes 7688 | tf_op jit(solution)/shard_map/while/body/eval_jaxpr/ppermute | solution.py:17
  139.2 6.4 %collective-permute-start = (f32[5,128]{1,0:T(8,128)S(1)}, f32[5,128]{1,0:T(8,128)S(1)}, u32[]{:S(2)}, u32[]{:S(2)}) collective-permute-start(f32[5,128]{1,0:T(8,128)S(1)} %get-tuple-element.302), channel_id=1, source_target_pairs={{0,16},{16,32},{32,48},{48,64},{64,80},{80,96},{96,112},{112,128},... | collective-permute-start | bytes 7688 | tf_op jit(solution)/shard_map/while/body/eval_jaxpr/ppermute | solution.py:17
  146.2 6.4 %collective-permute-start = (f32[5,128]{1,0:T(8,128)S(1)}, f32[5,128]{1,0:T(8,128)S(1)}, u32[]{:S(2)}, u32[]{:S(2)}) collective-permute-start(f32[5,128]{1,0:T(8,128)S(1)} %get-tuple-element.302), channel_id=1, source_target_pairs={{0,16},{16,32},{32,48},{48,64},{64,80},{80,96},{96,112},{112,128},... | collective-permute-start | bytes 7688 | tf_op jit(solution)/shard_map/while/body/eval_jaxpr/ppermute | solution.py:17
  153.2 6.5 %collective-permute-start = (f32[5,128]{1,0:T(8,128)S(1)}, f32[5,128]{1,0:T(8,128)S(1)}, u32[]{:S(2)}, u32[]{:S(2)}) collective-permute-start(f32[5,128]{1,0:T(8,128)S(1)} %get-tuple-element.302), channel_id=1, source_target_pairs={{0,16},{16,32},{32,48},{48,64},{64,80},{80,96},{96,112},{112,128},... | collective-permute-start | bytes 7688 | tf_op jit(solution)/shard_map/while/body/eval_jaxpr/ppermute | solution.py:17
  160.3 6.4 %collective-permute-start = (f32[5,128]{1,0:T(8,128)S(1)}, f32[5,128]{1,0:T(8,128)S(1)}, u32[]{:S(2)}, u32[]{:S(2)}) collective-permute-start(f32[5,128]{1,0:T(8,128)S(1)} %get-tuple-element.302), channel_id=1, source_target_pairs={{0,16},{16,32},{32,48},{48,64},{64,80},{80,96},{96,112},{112,128},... | collective-permute-start | bytes 7688 | tf_op jit(solution)/shard_map/while/body/eval_jaxpr/ppermute | solution.py:17
  167.4 6.4 %collective-permute-start = (f32[5,128]{1,0:T(8,128)S(1)}, f32[5,128]{1,0:T(8,128)S(1)}, u32[]{:S(2)}, u32[]{:S(2)}) collective-permute-start(f32[5,128]{1,0:T(8,128)S(1)} %get-tuple-element.302), channel_id=1, source_target_pairs={{0,16},{16,32},{32,48},{48,64},{64,80},{80,96},{96,112},{112,128},... | collective-permute-start | bytes 7688 | tf_op jit(solution)/shard_map/while/body/eval_jaxpr/ppermute | solution.py:17
  174.4 6.4 %collective-permute-start = (f32[5,128]{1,0:T(8,128)S(1)}, f32[5,128]{1,0:T(8,128)S(1)}, u32[]{:S(2)}, u32[]{:S(2)}) collective-permute-start(f32[5,128]{1,0:T(8,128)S(1)} %get-tuple-element.302), channel_id=1, source_target_pairs={{0,16},{16,32},{32,48},{48,64},{64,80},{80,96},{96,112},{112,128},... | collective-permute-start | bytes 7688 | tf_op jit(solution)/shard_map/while/body/eval_jaxpr/ppermute | solution.py:17
  181.4 6.4 %collective-permute-start = (f32[5,128]{1,0:T(8,128)S(1)}, f32[5,128]{1,0:T(8,128)S(1)}, u32[]{:S(2)}, u32[]{:S(2)}) collective-permute-start(f32[5,128]{1,0:T(8,128)S(1)} %get-tuple-element.302), channel_id=1, source_target_pairs={{0,16},{16,32},{32,48},{48,64},{64,80},{80,96},{96,112},{112,128},... | collective-permute-start | bytes 7688 | tf_op jit(solution)/shard_map/while/body/eval_jaxpr/ppermute | solution.py:17
  188.5 6.4 %collective-permute-start = (f32[5,128]{1,0:T(8,128)S(1)}, f32[5,128]{1,0:T(8,128)S(1)}, u32[]{:S(2)}, u32[]{:S(2)}) collective-permute-start(f32[5,128]{1,0:T(8,128)S(1)} %get-tuple-element.302), channel_id=1, source_target_pairs={{0,16},{16,32},{32,48},{48,64},{64,80},{80,96},{96,112},{112,128},... | collective-permute-start | bytes 7688 | tf_op jit(solution)/shard_map/while/body/eval_jaxpr/ppermute | solution.py:17
  195.5 6.4 %collective-permute-start = (f32[5,128]{1,0:T(8,128)S(1)}, f32[5,128]{1,0:T(8,128)S(1)}, u32[]{:S(2)}, u32[]{:S(2)}) collective-permute-start(f32[5,128]{1,0:T(8,128)S(1)} %get-tuple-element.302), channel_id=1, source_target_pairs={{0,16},{16,32},{32,48},{48,64},{64,80},{80,96},{96,112},{112,128},... | collective-permute-start | bytes 7688 | tf_op jit(solution)/shard_map/while/body/eval_jaxpr/ppermute | solution.py:17
  202.6 6.4 %collective-permute-start = (f32[5,128]{1,0:T(8,128)S(1)}, f32[5,128]{1,0:T(8,128)S(1)}, u32[]{:S(2)}, u32[]{:S(2)}) collective-permute-start(f32[5,128]{1,0:T(8,128)S(1)} %get-tuple-element.302), channel_id=1, source_target_pairs={{0,16},{16,32},{32,48},{48,64},{64,80},{80,96},{96,112},{112,128},... | collective-permute-start | bytes 7688 | tf_op jit(solution)/shard_map/while/body/eval_jaxpr/ppermute | solution.py:17
  209.6 6.4 %collective-permute-start = (f32[5,128]{1,0:T(8,128)S(1)}, f32[5,128]{1,0:T(8,128)S(1)}, u32[]{:S(2)}, u32[]{:S(2)}) collective-permute-start(f32[5,128]{1,0:T(8,128)S(1)} %get-tuple-element.302), channel_id=1, source_target_pairs={{0,16},{16,32},{32,48},{48,64},{64,80},{80,96},{96,112},{112,128},... | collective-permute-start | bytes 7688 | tf_op jit(solution)/shard_map/while/body/eval_jaxpr/ppermute | solution.py:17
  216.7 6.4 %collective-permute-start = (f32[5,128]{1,0:T(8,128)S(1)}, f32[5,128]{1,0:T(8,128)S(1)}, u32[]{:S(2)}, u32[]{:S(2)}) collective-permute-start(f32[5,128]{1,0:T(8,128)S(1)} %get-tuple-element.302), channel_id=1, source_target_pairs={{0,16},{16,32},{32,48},{48,64},{64,80},{80,96},{96,112},{112,128},... | collective-permute-start | bytes 7688 | tf_op jit(solution)/shard_map/while/body/eval_jaxpr/ppermute | solution.py:17
  226.1 6.7 %collective-permute-start.1 = (f32[5,128]{1,0:T(8,128)S(1)}, f32[5,128]{1,0:T(8,128)S(1)}, u32[]{:S(2)}, u32[]{:S(2)}) collective-permute-start(f32[5,128]{1,0:T(8,128)S(1)} %get-tuple-element.320), channel_id=1, source_target_pairs={{16,0},{32,16},{48,32},{64,48},{80,64},{96,80},{112,96},{128,112},... | collective-permute-start | bytes 7688 | tf_op jit(solution)/shard_map/while/body/eval_jaxpr/ppermute | solution.py:17
  233.4 6.4 %collective-permute-start.1 = (f32[5,128]{1,0:T(8,128)S(1)}, f32[5,128]{1,0:T(8,128)S(1)}, u32[]{:S(2)}, u32[]{:S(2)}) collective-permute-start(f32[5,128]{1,0:T(8,128)S(1)} %get-tuple-element.320), channel_id=1, source_target_pairs={{16,0},{32,16},{48,32},{64,48},{80,64},{96,80},{112,96},{128,112},... | collective-permute-start | bytes 7688 | tf_op jit(solution)/shard_map/while/body/eval_jaxpr/ppermute | solution.py:17
  240.4 6.4 %collective-permute-start.1 = (f32[5,128]{1,0:T(8,128)S(1)}, f32[5,128]{1,0:T(8,128)S(1)}, u32[]{:S(2)}, u32[]{:S(2)}) collective-permute-start(f32[5,128]{1,0:T(8,128)S(1)} %get-tuple-element.320), channel_id=1, source_target_pairs={{16,0},{32,16},{48,32},{64,48},{80,64},{96,80},{112,96},{128,112},... | collective-permute-start | bytes 7688 | tf_op jit(solution)/shard_map/while/body/eval_jaxpr/ppermute | solution.py:17
  247.4 6.4 %collective-permute-start.1 = (f32[5,128]{1,0:T(8,128)S(1)}, f32[5,128]{1,0:T(8,128)S(1)}, u32[]{:S(2)}, u32[]{:S(2)}) collective-permute-start(f32[5,128]{1,0:T(8,128)S(1)} %get-tuple-element.320), channel_id=1, source_target_pairs={{16,0},{32,16},{48,32},{64,48},{80,64},{96,80},{112,96},{128,112},... | collective-permute-start | bytes 7688 | tf_op jit(solution)/shard_map/while/body/eval_jaxpr/ppermute | solution.py:17
  254.5 6.4 %collective-permute-start.1 = (f32[5,128]{1,0:T(8,128)S(1)}, f32[5,128]{1,0:T(8,128)S(1)}, u32[]{:S(2)}, u32[]{:S(2)}) collective-permute-start(f32[5,128]{1,0:T(8,128)S(1)} %get-tuple-element.320), channel_id=1, source_target_pairs={{16,0},{32,16},{48,32},{64,48},{80,64},{96,80},{112,96},{128,112},... | collective-permute-start | bytes 7688 | tf_op jit(solution)/shard_map/while/body/eval_jaxpr/ppermute | solution.py:17
  261.5 6.4 %collective-permute-start.1 = (f32[5,128]{1,0:T(8,128)S(1)}, f32[5,128]{1,0:T(8,128)S(1)}, u32[]{:S(2)}, u32[]{:S(2)}) collective-permute-start(f32[5,128]{1,0:T(8,128)S(1)} %get-tuple-element.320), channel_id=1, source_target_pairs={{16,0},{32,16},{48,32},{64,48},{80,64},{96,80},{112,96},{128,112},... | collective-permute-start | bytes 7688 | tf_op jit(solution)/shard_map/while/body/eval_jaxpr/ppermute | solution.py:17
  268.6 6.4 %collective-permute-start.1 = (f32[5,128]{1,0:T(8,128)S(1)}, f32[5,128]{1,0:T(8,128)S(1)}, u32[]{:S(2)}, u32[]{:S(2)}) collective-permute-start(f32[5,128]{1,0:T(8,128)S(1)} %get-tuple-element.320), channel_id=1, source_target_pairs={{16,0},{32,16},{48,32},{64,48},{80,64},{96,80},{112,96},{128,112},... | collective-permute-start | bytes 7688 | tf_op jit(solution)/shard_map/while/body/eval_jaxpr/ppermute | solution.py:17
  275.6 6.4 %collective-permute-start.1 = (f32[5,128]{1,0:T(8,128)S(1)}, f32[5,128]{1,0:T(8,128)S(1)}, u32[]{:S(2)}, u32[]{:S(2)}) collective-permute-start(f32[5,128]{1,0:T(8,128)S(1)} %get-tuple-element.320), channel_id=1, source_target_pairs={{16,0},{32,16},{48,32},{64,48},{80,64},{96,80},{112,96},{128,112},... | collective-permute-start | bytes 7688 | tf_op jit(solution)/shard_map/while/body/eval_jaxpr/ppermute | solution.py:17
  282.7 6.4 %collective-permute-start.1 = (f32[5,128]{1,0:T(8,128)S(1)}, f32[5,128]{1,0:T(8,128)S(1)}, u32[]{:S(2)}, u32[]{:S(2)}) collective-permute-start(f32[5,128]{1,0:T(8,128)S(1)} %get-tuple-element.320), channel_id=1, source_target_pairs={{16,0},{32,16},{48,32},{64,48},{80,64},{96,80},{112,96},{128,112},... | collective-permute-start | bytes 7688 | tf_op jit(solution)/shard_map/while/body/eval_jaxpr/ppermute | solution.py:17
  289.7 6.4 %collective-permute-start.1 = (f32[5,128]{1,0:T(8,128)S(1)}, f32[5,128]{1,0:T(8,128)S(1)}, u32[]{:S(2)}, u32[]{:S(2)}) collective-permute-start(f32[5,128]{1,0:T(8,128)S(1)} %get-tuple-element.320), channel_id=1, source_target_pairs={{16,0},{32,16},{48,32},{64,48},{80,64},{96,80},{112,96},{128,112},... | collective-permute-start | bytes 7688 | tf_op jit(solution)/shard_map/while/body/eval_jaxpr/ppermute | solution.py:17
  303.8 6.6 %collective-permute-start.1 = (f32[5,128]{1,0:T(8,128)S(1)}, f32[5,128]{1,0:T(8,128)S(1)}, u32[]{:S(2)}, u32[]{:S(2)}) collective-permute-start(f32[5,128]{1,0:T(8,128)S(1)} %get-tuple-element.320), channel_id=1, source_target_pairs={{16,0},{32,16},{48,32},{64,48},{80,64},{96,80},{112,96},{128,112},... | collective-permute-start | bytes 7688 | tf_op jit(solution)/shard_map/while/body/eval_jaxpr/ppermute | solution.py:17
  310.9 6.4 %collective-permute-start.1 = (f32[5,128]{1,0:T(8,128)S(1)}, f32[5,128]{1,0:T(8,128)S(1)}, u32[]{:S(2)}, u32[]{:S(2)}) collective-permute-start(f32[5,128]{1,0:T(8,128)S(1)} %get-tuple-element.320), channel_id=1, source_target_pairs={{16,0},{32,16},{48,32},{64,48},{80,64},{96,80},{112,96},{128,112},... | collective-permute-start | bytes 7688 | tf_op jit(solution)/shard_map/while/body/eval_jaxpr/ppermute | solution.py:17
  325.0 6.4 %collective-permute-start.1 = (f32[5,128]{1,0:T(8,128)S(1)}, f32[5,128]{1,0:T(8,128)S(1)}, u32[]{:S(2)}, u32[]{:S(2)}) collective-permute-start(f32[5,128]{1,0:T(8,128)S(1)} %get-tuple-element.320), channel_id=1, source_target_pairs={{16,0},{32,16},{48,32},{64,48},{80,64},{96,80},{112,96},{128,112},... | collective-permute-start | bytes 7688 | tf_op jit(solution)/shard_map/while/body/eval_jaxpr/ppermute | solution.py:17
  339.1 6.4 %collective-permute-start.1 = (f32[5,128]{1,0:T(8,128)S(1)}, f32[5,128]{1,0:T(8,128)S(1)}, u32[]{:S(2)}, u32[]{:S(2)}) collective-permute-start(f32[5,128]{1,0:T(8,128)S(1)} %get-tuple-element.320), channel_id=1, source_target_pairs={{16,0},{32,16},{48,32},{64,48},{80,64},{96,80},{112,96},{128,112},... | collective-permute-start | bytes 7688 | tf_op jit(solution)/shard_map/while/body/eval_jaxpr/ppermute | solution.py:17
  360.2 6.4 %collective-permute-start.1 = (f32[5,128]{1,0:T(8,128)S(1)}, f32[5,128]{1,0:T(8,128)S(1)}, u32[]{:S(2)}, u32[]{:S(2)}) collective-permute-start(f32[5,128]{1,0:T(8,128)S(1)} %get-tuple-element.320), channel_id=1, source_target_pairs={{16,0},{32,16},{48,32},{64,48},{80,64},{96,80},{112,96},{128,112},... | collective-permute-start | bytes 7688 | tf_op jit(solution)/shard_map/while/body/eval_jaxpr/ppermute | solution.py:17
  374.3 6.4 %collective-permute-start.1 = (f32[5,128]{1,0:T(8,128)S(1)}, f32[5,128]{1,0:T(8,128)S(1)}, u32[]{:S(2)}, u32[]{:S(2)}) collective-permute-start(f32[5,128]{1,0:T(8,128)S(1)} %get-tuple-element.320), channel_id=1, source_target_pairs={{16,0},{32,16},{48,32},{64,48},{80,64},{96,80},{112,96},{128,112},... | collective-permute-start | bytes 7688 | tf_op jit(solution)/shard_map/while/body/eval_jaxpr/ppermute | solution.py:17
  409.5 6.5 %collective-permute-start.1 = (f32[5,128]{1,0:T(8,128)S(1)}, f32[5,128]{1,0:T(8,128)S(1)}, u32[]{:S(2)}, u32[]{:S(2)}) collective-permute-start(f32[5,128]{1,0:T(8,128)S(1)} %get-tuple-element.320), channel_id=1, source_target_pairs={{16,0},{32,16},{48,32},{64,48},{80,64},{96,80},{112,96},{128,112},... | collective-permute-start | bytes 7688 | tf_op jit(solution)/shard_map/while/body/eval_jaxpr/ppermute | solution.py:17
  430.7 6.4 %collective-permute-start.1 = (f32[5,128]{1,0:T(8,128)S(1)}, f32[5,128]{1,0:T(8,128)S(1)}, u32[]{:S(2)}, u32[]{:S(2)}) collective-permute-start(f32[5,128]{1,0:T(8,128)S(1)} %get-tuple-element.320), channel_id=1, source_target_pairs={{16,0},{32,16},{48,32},{64,48},{80,64},{96,80},{112,96},{128,112},... | collective-permute-start | bytes 7688 | tf_op jit(solution)/shard_map/while/body/eval_jaxpr/ppermute | solution.py:17
  511.6 94.8 %all-to-all-start = ((f32[80,5,128]{2,1,0:T(8,128)}), f32[80,5,128]{2,1,0:T(8,128)S(1)}, u32[]{:S(2)}, u32[]{:S(2)}) async-start(f32[80,5,128]{2,1,0:T(8,128)} %copy.120), calls=%async_computation | async-start | bytes 655360 | tf_op jit(solution)/shard_map/all_to_all | solution.py:120
  (78 other events, 633.9 us)
where the time goes:
time: 609 us; the launch traced here: 607 us
  starting transfers between devices  313 us (51%)
  waiting for transfers between devices  177 us (29%)
  local copies, waits for them, and re-layouts  99.4 us (16%)
  other arithmetic  13.7 us (2%)
    ppermute x62, starting transfers between devices, passed_along(): lax.ppermute(value, axis, [(source, source + steps) for source in range(f...  232 us
    ppermute x62, waiting for transfers between devices, passed_along(): lax.ppermute(value, axis, [(source, source + steps) for source in range(f...  165 us
    all_to_all x1, starting transfers between devices, body(): lax.all_to_all(outgoing, 'valve', split_axis=0, concat_axis=0, tiled=True)  81.7 us
    gather x1, local copies, waits for them, and re-layouts, body(): picked = local_cells[:, donor_cells]  54.4 us
    while x124, local copies, waits for them, and re-layouts  34.9 us
    all_to_all x1, waiting for transfers between devices, body(): lax.all_to_all(outgoing, 'valve', split_axis=0, concat_axis=0, tiled=True)  12.5 us
  transfers between devices with their start and end apart: 63, of which 63 were waited for; matrix products, arithmetic and copies ran while one was open for 0% of the time, Pallas kernels for 0%

commit v1 on v0

v1 whole, which is shorter than its diff:
```python
import functools

import jax
import jax.numpy as jnp
from jax import lax
from jax.experimental import pallas as pl
from jax.experimental.pallas import tpu as pltpu
from jax.sharding import PartitionSpec as P

NY = 8
PLANES = 8
CELLS = 128
POINTS = 128
CAPACITY = 5
ROWS = 32
MESH = pl.DeviceIdType.MESH
VMEM = pltpu.VMEM
F32 = jnp.float32


def compose(left, right):
    total = left[:, 0][:, None] * right[0][None]
    for c in range(1, 5):
        total = total + left[:, c][:, None] * right[c][None]
    return total


def apply(matrices, vectors):
    total = matrices[:, 0] * vectors[0][None]
    for c in range(1, 5):
        total = total + matrices[:, c] * vectors[c][None]
    return total


def shifted(value, amount):
    shape = value.shape
    flat = value.reshape((-1,) + shape[-2:])
    return pltpu.roll(flat, amount % shape[-2], 1).reshape(shape)


def forward_scan(matrices, offsets):
    row = lax.broadcasted_iota(jnp.int32, (8, CELLS), 0)
    for step in (1, 2, 4):
        live = row >= step
        new_offsets = offsets + apply(matrices, shifted(offsets, step))
        new_matrices = compose(matrices, shifted(matrices, step))
        offsets = jnp.where(live[None], new_offsets, offsets)
        matrices = jnp.where(live[None, None], new_matrices, matrices)
    return matrices, offsets


def backward_matrices(matrices, levels_ref):
    row = lax.broadcasted_iota(jnp.int32, (8, CELLS), 0)
    for level, step in enumerate((1, 2, 4)):
        live = row < 8 - step
        levels_ref[level] = jnp.where(live[None, None], matrices, 0.0)
        matrices = jnp.where(live[None, None], compose(matrices, shifted(matrices, -step)), matrices)
    return matrices


def backward_offsets(levels_ref, offsets):
    for level, step in enumerate((1, 2, 4)):
        offsets = offsets + apply(levels_ref[level], shifted(offsets, -step))
    return offsets


def picked_row(values, index):
    row = lax.broadcasted_iota(jnp.int32, (8, CELLS), 0)
    kept = jnp.where((row == index)[None], values, 0.0)
    for step in (1, 2, 4):
        kept = kept + shifted(kept, step)
    return kept


def sweep_kernel(
    nx,
    rhs_ref,
    diag_ref,
    lower_ref,
    upper_ref,
    update_ref,
    low_out,
    low_all,
    low_total,
    low_rows,
    up_out,
    up_all,
    up_total,
    up_rows,
    off_out,
    off_all,
    off_total,
    off_rows,
    plane_levels,
    row_levels,
    y_send,
    y_recv,
    x_send,
    x_recv,
):
    bulk = lax.axis_index("bulk")
    my_x = bulk // NY
    my_y = bulk % NY

    def y_peer(step):
        return {"bulk": my_x * NY + (my_y + step) % NY}

    def x_peer(step):
        return {"bulk": ((my_x + step) % nx) * NY + my_y}

    barrier = pltpu.get_barrier_semaphore()
    for step in range(1, NY):
        pl.semaphore_signal(barrier, inc=1, device_id=y_peer(step), device_id_type=MESH)
    for step in range(1, nx):
        pl.semaphore_signal(barrier, inc=1, device_id=x_peer(step), device_id_type=MESH)

    def place(ref, index, rows):
        return ref.at[pl.ds(pl.multiple_of(index * rows, 8), rows), :]

    def send_y(stage, source, target, rows):
        copies = []
        for step in (4, 3, 5, 2, 6, 1, 7):
            copy = pltpu.make_async_remote_copy(
                src_ref=source,
                dst_ref=place(target, my_y, rows),
                send_sem=y_send.at[stage, step - 1],
                recv_sem=y_recv.at[stage, step - 1],
                device_id=y_peer(step),
                device_id_type=MESH,
            )
            copy.start()
            copies.append(copy)
        return copies

    def send_x(stage, source, target, rows):
        copies = []
        for step in range(1, nx):
            copy = pltpu.make_async_remote_copy(
                src_ref=source,
                dst_ref=place(target, my_x, rows),
                send_sem=x_send.at[stage, step - 1],
                recv_sem=x_recv.at[stage, step - 1],
                device_id=x_peer(step),
                device_id_type=MESH,
            )
            copy.start()
            copies.append(copy)
        return copies

    def arrive(copies):
        for copy in copies:
            copy.wait_recv()

    def put(ref, first, value, row):
        for index in range(value.shape[0]):
            ref[first + index : first + index + 1, :] = value[index, row : row + 1, :]

    def gathered(ref, first, count, stride):
        return jnp.stack([ref[pl.ds(first + index, 8, stride=stride), :] for index in range(count)])

    diag = diag_ref[...]
    low_matrices, low_offsets = forward_scan(-compose(diag, lower_ref[...]), apply(diag, rhs_ref[...]))
    put(low_out, 0, low_matrices.reshape(25, PLANES, CELLS), PLANES - 1)
    put(low_out, 25, low_offsets, PLANES - 1)
    place(low_all, my_y, ROWS)[...] = low_out[...]
    pl.semaphore_wait(barrier, NY + nx - 2)
    low_y = send_y(0, low_out, low_all, ROWS)

    up_matrices = backward_matrices(-compose(diag, upper_ref[...]), plane_levels)
    put(up_out, 0, up_matrices.reshape(25, PLANES, CELLS), 0)
    place(up_all, my_y, ROWS)[...] = up_out[...]
    up_y = send_y(1, up_out, up_all, ROWS)

    arrive(low_y)
    row_matrices, row_offsets = forward_scan(
        gathered(low_all, 0, 25, ROWS).reshape(5, 5, 8, CELLS), gathered(low_all, 25, 5, ROWS)
    )
    put(low_total, 0, row_matrices.reshape(25, 8, CELLS), 7)
    put(low_total, 25, row_offsets, 7)
    low_x = send_x(0, low_total, low_rows, ROWS)

    arrive(up_y)
    row_up = backward_matrices(gathered(up_all, 0, 25, ROWS).reshape(5, 5, 8, CELLS), row_levels)
    put(up_total, 0, row_up.reshape(25, 8, CELLS), 0)
    up_x = send_x(1, up_total, up_rows, ROWS)

    place(low_rows, my_x, ROWS)[...] = low_total[...]
    place(up_rows, my_x, ROWS)[...] = up_total[...]

    def chain(rows, offsets_of, order, passes):
        state = [jnp.zeros((1, CELLS), F32) for _ in range(5)]
        for x in order:
            offsets = offsets_of(x)
            new_state = []
            for a in range(5):
                value = offsets[a]
                for b in range(5):
                    at = x * ROWS + a * 5 + b
                    value = value + rows[at : at + 1, :] * state[b]
                new_state.append(value)
            keep = passes(x)
            state = [jnp.where(keep, new, old) for new, old in zip(new_state, state)]
        return jnp.stack([jnp.broadcast_to(value, (8, CELLS)) for value in state])

    arrive(low_x)
    entering = chain(
        low_rows,
        lambda x: [low_rows[x * ROWS + 25 + a : x * ROWS + 26 + a, :] for a in range(5)],
        range(nx - 1),
        lambda x: x < my_x,
    )
    leaving = row_offsets + apply(row_matrices, entering)
    incoming = jnp.where(my_y == 0, entering, picked_row(leaving, my_y - 1))
    starred = low_offsets + apply(low_matrices, incoming)

    partial = backward_offsets(plane_levels, starred)
    put(off_out, 0, partial, 0)
    off_y = send_y(2, off_out, off_all, 8)
    place(off_all, my_y, 8)[...] = off_out[...]
    arrive(up_x)
    arrive(off_y)
    row_partial = backward_offsets(row_levels, gathered(off_all, 0, 5, 8))
    put(off_total, 0, row_partial, 0)
    off_x = send_x(2, off_total, off_rows, 8)
    place(off_rows, my_x, 8)[...] = off_total[...]
    arrive(off_x)
    entering = chain(
        up_rows,
        lambda x: [off_rows[x * 8 + a : x * 8 + a + 1, :] for a in range(5)],
        range(nx - 1, 0, -1),
        lambda x: x > my_x,
    )
    leaving = row_partial + apply(row_up, entering)
    incoming = jnp.where(my_y == NY - 1, entering, picked_row(leaving, my_y + 1))
    update_ref[...] = partial + apply(up_matrices, incoming)

    for copies in (low_y, up_y, low_x, up_x, off_y, off_x):
        for copy in copies:
            copy.wait_send()


def sweeps(nx, rhs, diag, lower, upper):
    return pl.pallas_call(
        functools.partial(sweep_kernel, nx),
        out_shape=jax.ShapeDtypeStruct((5, PLANES, CELLS), F32),
        in_specs=[pl.BlockSpec(memory_space=VMEM)] * 4,
        out_specs=pl.BlockSpec(memory_space=VMEM),
        scratch_shapes=[
            VMEM((ROWS, CELLS), F32),
            VMEM((NY * ROWS, CELLS), F32),
            VMEM((ROWS, CELLS), F32),
            VMEM((nx * ROWS, CELLS), F32),
            VMEM((ROWS, CELLS), F32),
            VMEM((NY * ROWS, CELLS), F32),
            VMEM((ROWS, CELLS), F32),
            VMEM((nx * ROWS, CELLS), F32),
            VMEM((8, CELLS), F32),
            VMEM((NY * 8, CELLS), F32),
            VMEM((8, CELLS), F32),
            VMEM((nx * 8, CELLS), F32),
            VMEM((3, 5, 5, 8, CELLS), F32),
            VMEM((3, 5, 5, 8, CELLS), F32),
            pltpu.SemaphoreType.DMA((3, NY - 1)),
            pltpu.SemaphoreType.DMA((3, NY - 1)),
            pltpu.SemaphoreType.DMA((3, max(nx - 1, 1))),
            pltpu.SemaphoreType.DMA((3, max(nx - 1, 1))),
        ],
        compiler_params=pltpu.CompilerParams(collective_id=0, has_side_effects=True),
    )(rhs, diag, lower, upper)


def fringe_kernel(
    nv,
    count_ref,
    owner_ref,
    owner_row_ref,
    update_ref,
    index_ref,
    weight_ref,
    out_ref,
    table,
    values,
    outgoing,
    arrived,
    send_sem,
    recv_sem,
):
    me = lax.axis_index("valve")
    blocks = index_ref.shape[0]
    barrier = pltpu.get_barrier_semaphore()
    for step in range(1, nv):
        pl.semaphore_signal(barrier, inc=1, device_id={"valve": (me + step) % nv}, device_id_type=MESH)

    for c in range(5):
        for plane in range(PLANES):
            table[c, plane] = jnp.broadcast_to(update_ref[c, plane : plane + 1, :], (8, CELLS))
    lane = lax.broadcasted_iota(jnp.int32, (1, POINTS), 1)

    def interpolate(block, carry):
        donors = index_ref[block]
        weights = weight_ref[block]
        cell = donors & (CELLS - 1)
        plane_of = donors >> 7
        live = lane < count_ref[0, block]
        here = [plane_of == plane for plane in range(PLANES)]
        for c in range(5):
            picked = jnp.take_along_axis(table[c, 0], cell, axis=1, mode="promise_in_bounds")
            for plane in range(1, PLANES):
                other = jnp.take_along_axis(table[c, plane], cell, axis=1, mode="promise_in_bounds")
                picked = jnp.where(here[plane], other, picked)
            total = jnp.sum(weights * picked, axis=0, keepdims=True)
            values[c, pl.ds(block, 1), :] = jnp.where(live, total, 0.0)
        return carry

    lax.fori_loop(0, blocks, interpolate, 0)

    owner = owner_row_ref[...]
    position = lax.broadcasted_iota(jnp.int32, (1, blocks), 1)
    rank = jnp.zeros((1, blocks), jnp.int32)
    for earlier in range(blocks):
        same = (owner == owner_ref[0, earlier]) & (position > earlier)
        rank = rank + jnp.where(same, 1, 0)
    target = owner * 8 + rank
    slot = lax.broadcasted_iota(jnp.int32, (nv * 8, blocks), 0)
    placement = jnp.where(slot == target, 1.0, 0.0).astype(F32)
    for c in range(5):
        rows = jnp.dot(placement, values[c], precision=lax.Precision.HIGHEST, preferred_element_type=F32)
        outgoing[:, c] = rows.reshape(nv, 8, POINTS)

    pl.semaphore_wait(barrier, nv - 1)
    copies = []
    for step in range(1, nv):
        peer = (me + step) % nv
        copy = pltpu.make_async_remote_copy(
            src_ref=outgoing.at[peer],
            dst_ref=arrived.at[me],
            send_sem=send_sem.at[step - 1],
            recv_sem=recv_sem.at[step - 1],
            device_id={"valve": peer},
            device_id_type=MESH,
        )
        copy.start()
        copies.append(copy)
    arrived[me] = outgoing[me]
    for copy in copies:
        copy.wait_recv()
    for source in range(nv):
        for c in range(5):
            out_ref[c, source * CAPACITY : (source + 1) * CAPACITY, :] = arrived[source, c, 0:CAPACITY, :]
    for copy in copies:
        copy.wait_send()


def fringe(nv, count, owner, update, index, weight):
    blocks = index.shape[0]
    smem = pl.BlockSpec(memory_space=pltpu.SMEM)
    vmem = pl.BlockSpec(memory_space=VMEM)
    return pl.pallas_call(
        functools.partial(fringe_kernel, nv),
        out_shape=jax.ShapeDtypeStruct((5, nv * CAPACITY, POINTS), F32),
        in_specs=[smem, smem, vmem, vmem, vmem, vmem],
        out_specs=vmem,
        scratch_shapes=[
            VMEM((5, PLANES, 8, CELLS), F32),
            VMEM((5, blocks, POINTS), F32),
            VMEM((nv, 5, 8, POINTS), F32),
            VMEM((nv, 5, 8, POINTS), F32),
            pltpu.SemaphoreType.DMA((nv - 1,)),
            pltpu.SemaphoreType.DMA((nv - 1,)),
        ],
        compiler_params=pltpu.CompilerParams(collective_id=1, has_side_effects=True),
    )(count, owner, owner, update, index, weight)


def solution(mesh):
    nx = mesh.shape["bulk"] // NY
    nv = mesh.shape["valve"]

    def body(rhs, diag, lower, upper, index, weight, count, owner):
        update = sweeps(nx, rhs, diag, lower, upper)
        rows = fringe(nv, count, owner, update, index[0], weight[0])
        return update, jnp.transpose(rows, (1, 0, 2))[None]

    in_specs = (
        P(None, "bulk", "valve"),
        P(None, None, "bulk", "valve"),
        P(None, None, "bulk", "valve"),
        P(None, None, "bulk", "valve"),
        P("bulk", "valve", None, None),
        P("bulk", "valve", None, None),
        P("bulk", "valve"),
        P("bulk", "valve"),
    )
    out_specs = (P(None, "bulk", "valve"), P("bulk", "valve", None, None))
    return jax.shard_map(body, mesh=mesh, in_specs=in_specs, out_specs=out_specs, check_vma=False)
```

time: 609 us -> 52 us (0.09)
  the two profiles are of different devices: /device:TPU:57 before, /device:TPU:1 now
where the time goes in v1:
time: 52 us; the launch traced here: 51.7 us
  Pallas kernels  48.8 us (94%)
  local copies, waits for them, and re-layouts  2.24 us (4%)
  between operations  0.66 us (1%)
    pallas_call x1, Pallas kernels, fringe(): pl.pallas_call(functools.partial(fringe_kernel, nv), out_shape=jax.ShapeD...  25 us
    pallas_call x1, Pallas kernels, sweeps(): pl.pallas_call(functools.partial(sweep_kernel, nx), out_shape=jax.ShapeDt...  23.9 us
    unnamed x4, local copies, waits for them, and re-layouts  2.24 us

profile of v1, /device:TPU:1, one launch (start us, length us, event | category | flops | bytes accessed | tf_op | source)
XLA Modules:
  0.0 51.7 jit_solution(8680368383135253323)
XLA Ops:
  0.6 23.9 %shard_map.95.update_ref = f32[5,8,128]{2,1,0:T(8,128)} custom-call(f32[5,8,128]{2,1,0:T(8,128)} %rhs_ref.1, f32[5,5,8,128]{3,2,1,0:T(8,128)} %diag_ref.1, f32[5,5,8,128]{3,2,1,0:T(8,128)} %lower_ref.1, f32[5,5,8,128]{3,2,1,0:T(8,128)} %upper_ref.1), custom_call_target="tpu_custom_call" | custom-call | tf_op jit(solution)/shard_map/pallas_call | solution.py:243
  24.5 0.0 copy-start
  24.5 25.0 %shard_map.96 = f32[5,80,128]{2,1,0:T(8,128)} custom-call(s32[1,16]{1,0:T(1,128)} %count_ref.1, s32[1,16]{1,0:T(1,128)} %owner_row_ref.1, s32[1,16]{1,0:T(1,128)} %owner_row_ref.1, f32[5,8,128]{2,1,0:T(8,128)} %shard_map.95.update_ref, s32[16,8,128]{2,1,0:T(8,128)} %bitcast.6, f32[16,8,128]{2,1,0:T(8,128)} %bitcast.7), custom_call_target="tpu_custom_call" | custom-call | tf_op jit(solution)/shard_map/pallas_call | solution.py:358
  49.5 0.0 copy-done
  49.5 0.6 %copy.12 = f32[5,8,128]{2,1,0:T(8,128)} copy(f32[5,8,128]{2,1,0:T(8,128)S(1)} %copy-done) | data formatting | bytes 40960
  50.1 1.6 %copy.13 = f32[1,80,5,128]{3,1,2,0:T(8,128)} copy(f32[1,80,5,128]{3,1,2,0:T(8,128)} %bitcast.5) | data formatting | bytes 409600
Async XLA Ops:
  24.5 25.0 %copy-start = (f32[5,8,128]{2,1,0:T(8,128)S(1)}, f32[5,8,128]{2,1,0:T(8,128)}, u32[]{:S(2)}) copy-start(f32[5,8,128]{2,1,0:T(8,128)} %shard_map.95.update_ref) | copy-start | bytes 61444

commit v2 on v1

--- a/solution.py
+++ b/solution.py
@@ -13,6 +13,7 @@
 POINTS = 128
 CAPACITY = 5
 ROWS = 32
+BLOCKS = 16
 MESH = pl.DeviceIdType.MESH
 VMEM = pltpu.VMEM
 F32 = jnp.float32
@@ -72,13 +73,27 @@
     return kept
 
 
-def sweep_kernel(
+def whole_kernel(
     nx,
+    nv,
+    rhs_hbm,
+    diag_hbm,
+    lower_hbm,
+    upper_hbm,
+    index_hbm,
+    weight_hbm,
+    count_hbm,
+    owner_hbm,
+    update_ref,
+    fringe_ref,
     rhs_ref,
     diag_ref,
     lower_ref,
     upper_ref,
-    update_ref,
+    index_ref,
+    weight_ref,
+    count_ref,
+    owner_ref,
     low_out,
     low_all,
     low_total,
@@ -93,11 +108,42 @@
     off_rows,
     plane_levels,
     row_levels,
+    table,
+    products,
+    select_first,
+    select_second,
+    select_third,
+    select_extra,
+    outgoing,
+    arrived,
+    extra_out,
+    extra_in,
+    load_sem,
     y_send,
     y_recv,
     x_send,
     x_recv,
+    v_send,
+    v_recv,
 ):
+    loads = []
+    for number, (source, target) in enumerate(
+        (
+            (diag_hbm, diag_ref),
+            (lower_hbm, lower_ref),
+            (rhs_hbm, rhs_ref),
+            (upper_hbm, upper_ref),
+            (owner_hbm, owner_ref),
+            (count_hbm, count_ref),
+            (weight_hbm, weight_ref),
+            (index_hbm, index_ref),
+        )
+    ):
+        load = pltpu.make_async_copy(source, target, load_sem.at[number])
+        load.start()
+        loads.append(load)
+    me = lax.axis_index("valve")
+    blocks = BLOCKS
     bulk = lax.axis_index("bulk")
     my_x = bulk // NY
     my_y = bulk % NY
@@ -113,6 +159,9 @@
         pl.semaphore_signal(barrier, inc=1, device_id=y_peer(step), device_id_type=MESH)
     for step in range(1, nx):
         pl.semaphore_signal(barrier, inc=1, device_id=x_peer(step), device_id_type=MESH)
+
+    for step in range(1, nv):
+        pl.semaphore_signal(barrier, inc=1, device_id={"valve": (me + step) % nv}, device_id_type=MESH)
 
     def place(ref, index, rows):
         return ref.at[pl.ds(pl.multiple_of(index * rows, 8), rows), :]
@@ -158,18 +207,48 @@
     def gathered(ref, first, count, stride):
         return jnp.stack([ref[pl.ds(first + index, 8, stride=stride), :] for index in range(count)])
 
+    for load in loads[:3]:
+        load.wait()
     diag = diag_ref[...]
     low_matrices, low_offsets = forward_scan(-compose(diag, lower_ref[...]), apply(diag, rhs_ref[...]))
     put(low_out, 0, low_matrices.reshape(25, PLANES, CELLS), PLANES - 1)
     put(low_out, 25, low_offsets, PLANES - 1)
     place(low_all, my_y, ROWS)[...] = low_out[...]
-    pl.semaphore_wait(barrier, NY + nx - 2)
+    pl.semaphore_wait(barrier, NY + nx + nv - 3)
     low_y = send_y(0, low_out, low_all, ROWS)
 
+    loads[3].wait()
     up_matrices = backward_matrices(-compose(diag, upper_ref[...]), plane_levels)
     put(up_out, 0, up_matrices.reshape(25, PLANES, CELLS), 0)
     place(up_all, my_y, ROWS)[...] = up_out[...]
     up_y = send_y(1, up_out, up_all, ROWS)
+
+    for load in loads[4:]:
+        load.wait()
+    lane = lax.broadcasted_iota(jnp.int32, (1, CELLS), 1)
+    block_of = lane >> 3
+    owner = jnp.zeros((1, CELLS), jnp.int32)
+    for block in range(blocks):
+        owner = jnp.where(block_of == block, owner_ref[0, block], owner)
+    rank = jnp.zeros((1, CELLS), jnp.int32)
+    for earlier in range(blocks):
+        same = (owner == owner_ref[0, earlier]) & (block_of > earlier)
+        rank = rank + jnp.where(same, 1, 0)
+    goal = owner * CAPACITY + rank
+    line = lax.broadcasted_iota(jnp.int32, (nv * 8, CELLS), 0)
+    for tile, (selection, first, last) in enumerate(
+        ((select_first, 0, 2), (select_second, 1, 4), (select_third, 3, 5))
+    ):
+        number = tile * 8 + (line & 7)
+        component = (number * 13) >> 6
+        wanted = (line >> 3) * CAPACITY + number - component * CAPACITY
+        for c in range(first, last):
+            hit = (component == c) & (wanted == goal)
+            selection[:, (c - first) * CELLS : (c - first + 1) * CELLS] = jnp.where(hit, 1.0, 0.0).astype(F32)
+    wanted = lax.broadcasted_iota(jnp.int32, (nv, CELLS), 0) * CAPACITY + CAPACITY - 1
+    select_extra[...] = jnp.where(wanted == goal, 1.0, 0.0).astype(F32)
+    for block in range(blocks):
+        weight_ref[block] = jnp.where(lane < count_ref[0, block], weight_ref[block], 0.0)
 
     arrive(low_y)
     row_matrices, row_offsets = forward_scan(
@@ -232,20 +311,116 @@
     )
     leaving = row_partial + apply(row_up, entering)
     incoming = jnp.where(my_y == NY - 1, entering, picked_row(leaving, my_y + 1))
-    update_ref[...] = partial + apply(up_matrices, incoming)
-
-    for copies in (low_y, up_y, low_x, up_x, off_y, off_x):
+    update = partial + apply(up_matrices, incoming)
+    update_ref[...] = update
+    for c in range(5):
+        for plane in range(PLANES):
+            table[c, plane] = jnp.broadcast_to(update[c, plane : plane + 1, :], (8, CELLS))
+
+    def interpolate(components):
+        def step(block, carry):
+            donors = index_ref[block]
+            weights = weight_ref[block]
+            cell = donors & (CELLS - 1)
+            plane_of = donors >> 7
+            here = [plane_of == plane for plane in range(PLANES)]
+            for c in components:
+                picked = jnp.take_along_axis(table[c, 0], cell, axis=1, mode="promise_in_bounds")
+                for plane in range(1, PLANES):
+                    other = jnp.take_along_axis(table[c, plane], cell, axis=1, mode="promise_in_bounds")
+                    picked = jnp.where(here[plane], other, picked)
+                products[c, pl.ds(pl.multiple_of(block * 8, 8), 8), :] = weights * picked
+            return carry
+
+        lax.fori_loop(0, blocks, step, 0, unroll=2)
+
+    def selected(selection, first, last):
+        total = None
+        for c in range(first, last):
+            part = jnp.dot(
+                selection[:, (c - first) * CELLS : (c - first + 1) * CELLS],
+                products[c],
+                precision=lax.Precision.HIGHEST,
+                preferred_element_type=F32,
+            )
+            total = part if total is None else total + part
+        return total
+
+    def send_v(stage, source_of, target_of):
+        copies = []
+        for step in sorted(range(1, nv), key=lambda step: -min(step, nv - step)):
+            peer = (me + step) % nv
+            copy = pltpu.make_async_remote_copy(
+                src_ref=source_of(peer),
+                dst_ref=target_of(me),
+                send_sem=v_send.at[stage, step - 1],
+                recv_sem=v_recv.at[stage, step - 1],
+                device_id={"valve": peer},
+                device_id_type=MESH,
+            )
+            copy.start()
+            copies.append(copy)
+        return copies
+
+    def exchange(tile, selection, first, last):
+        outgoing[tile] = selected(selection, first, last).reshape(nv, 8, POINTS)
+        copies = send_v(tile, lambda peer: outgoing.at[tile, peer], lambda mine: arrived.at[tile, mine])
+        arrived[tile, me] = outgoing[tile, me]
+        return copies
+
+    sent = []
+    interpolate((0, 1))
+    sent += exchange(0, select_first, 0, 2)
+    interpolate((2, 3))
+    sent += exchange(1, select_second, 1, 4)
+    interpolate((4,))
+    sent += exchange(2, select_third, 3, 5)
+    extra = selected(select_extra, 4, 5)
+    for device in range(nv):
+        extra_out[device] = extra[device : device + 1, :]
+    sent += send_v(3, lambda peer: extra_out.at[peer], lambda mine: extra_in.at[mine])
+    extra_in[me] = extra_out[me]
+
+    arrive(sent)
+    for source in range(nv):
+        base = source * CAPACITY
+        for c in range(5):
+            slot = 0
+            while slot < CAPACITY:
+                number = c * CAPACITY + slot
+                if number == 24:
+                    fringe_ref[c, base + slot : base + slot + 1, :] = extra_in[source]
+                    break
+                row = number % 8
+                count = min(CAPACITY - slot, 8 - row)
+                fringe_ref[c, base + slot : base + slot + count, :] = arrived[number // 8, source, row : row + count, :]
+                slot += count
+
+    for copies in (low_y, up_y, low_x, up_x, off_y, off_x, sent):
         for copy in copies:
             copy.wait_send()
 
 
-def sweeps(nx, rhs, diag, lower, upper):
+def whole(nx, nv, rhs, diag, lower, upper, index, weight, count, owner):
+    hbm = pl.BlockSpec(memory_space=pl.ANY)
+    vmem = pl.BlockSpec(memory_space=VMEM)
     return pl.pallas_call(
-        functools.partial(sweep_kernel, nx),
-        out_shape=jax.ShapeDtypeStruct((5, PLANES, CELLS), F32),
-        in_specs=[pl.BlockSpec(memory_space=VMEM)] * 4,
-        out_specs=pl.BlockSpec(memory_space=VMEM),
+        functools.partial(whole_kernel, nx, nv),
+        out_shape=(
+            jax.ShapeDtypeStruct((5, PLANES, CELLS), F32),
+            jax.ShapeDtypeStruct((5, nv * CAPACITY, POINTS), F32),
+        ),
+        in_specs=[hbm] * 8,
+        out_specs=(vmem, vmem),
         scratch_shapes=[
+            VMEM((5, PLANES, CELLS), F32),
+            VMEM((5, 5, PLANES, CELLS), F32),
+            VMEM((5, 5, PLANES, CELLS), F32),
+            VMEM((5, 5, PLANES, CELLS), F32),
+            VMEM((BLOCKS, 8, POINTS), jnp.int32),
+            VMEM((BLOCKS, 8, POINTS), F32),
+            pltpu.SMEM((1, BLOCKS), jnp.int32),
+            pltpu.SMEM((1, BLOCKS), jnp.int32),
             VMEM((ROWS, CELLS), F32),
             VMEM((NY * ROWS, CELLS), F32),
             VMEM((ROWS, CELLS), F32),
@@ -260,116 +435,26 @@
             VMEM((nx * 8, CELLS), F32),
             VMEM((3, 5, 5, 8, CELLS), F32),
             VMEM((3, 5, 5, 8, CELLS), F32),
+            VMEM((5, PLANES, 8, CELLS), F32),
+            VMEM((5, BLOCKS * 8, POINTS), F32),
+            VMEM((nv * 8, 2 * CELLS), F32),
+            VMEM((nv * 8, 3 * CELLS), F32),
+            VMEM((nv * 8, 2 * CELLS), F32),
+            VMEM((nv, CELLS), F32),
+            VMEM((3, nv, 8, POINTS), F32),
+            VMEM((3, nv, 8, POINTS), F32),
+            VMEM((nv, 1, POINTS), F32),
+            VMEM((nv, 1, POINTS), F32),
+            pltpu.SemaphoreType.DMA((8,)),
             pltpu.SemaphoreType.DMA((3, NY - 1)),
             pltpu.SemaphoreType.DMA((3, NY - 1)),
-            pltpu.SemaphoreType.DMA((3, max(nx - 1, 1))),
-            pltpu.SemaphoreType.DMA((3, max(nx - 1, 1))),
+            pltpu.SemaphoreType.DMA((3, nx - 1)),
+            pltpu.SemaphoreType.DMA((3, nx - 1)),
+            pltpu.SemaphoreType.DMA((4, nv - 1)),
+            pltpu.SemaphoreType.DMA((4, nv - 1)),
         ],
         compiler_params=pltpu.CompilerParams(collective_id=0, has_side_effects=True),
-    )(rhs, diag, lower, upper)
-
-
-def fringe_kernel(
-    nv,
-    count_ref,
-    owner_ref,
-    owner_row_ref,
-    update_ref,
-    index_ref,
-    weight_ref,
-    out_ref,
-    table,
-    values,
-    outgoing,
-    arrived,
-    send_sem,
-    recv_sem,
-):
-    me = lax.axis_index("valve")
-    blocks = index_ref.shape[0]
-    barrier = pltpu.get_barrier_semaphore()
-    for step in range(1, nv):
-        pl.semaphore_signal(barrier, inc=1, device_id={"valve": (me + step) % nv}, device_id_type=MESH)
-
-    for c in range(5):
-        for plane in range(PLANES):
-            table[c, plane] = jnp.broadcast_to(update_ref[c, plane : plane + 1, :], (8, CELLS))
-    lane = lax.broadcasted_iota(jnp.int32, (1, POINTS), 1)
-
-    def interpolate(block, carry):
-        donors = index_ref[block]
-        weights = weight_ref[block]
-        cell = donors & (CELLS - 1)
-        plane_of = donors >> 7
-        live = lane < count_ref[0, block]
-        here = [plane_of == plane for plane in range(PLANES)]
-        for c in range(5):
-            picked = jnp.take_along_axis(table[c, 0], cell, axis=1, mode="promise_in_bounds")
-            for plane in range(1, PLANES):
-                other = jnp.take_along_axis(table[c, plane], cell, axis=1, mode="promise_in_bounds")
-                picked = jnp.where(here[plane], other, picked)
-            total = jnp.sum(weights * picked, axis=0, keepdims=True)
-            values[c, pl.ds(block, 1), :] = jnp.where(live, total, 0.0)
-        return carry
-
-    lax.fori_loop(0, blocks, interpolate, 0)
-
-    owner = owner_row_ref[...]
-    position = lax.broadcasted_iota(jnp.int32, (1, blocks), 1)
-    rank = jnp.zeros((1, blocks), jnp.int32)
-    for earlier in range(blocks):
-        same = (owner == owner_ref[0, earlier]) & (position > earlier)
-        rank = rank + jnp.where(same, 1, 0)
-    target = owner * 8 + rank
-    slot = lax.broadcasted_iota(jnp.int32, (nv * 8, blocks), 0)
-    placement = jnp.where(slot == target, 1.0, 0.0).astype(F32)
-    for c in range(5):
-        rows = jnp.dot(placement, values[c], precision=lax.Precision.HIGHEST, preferred_element_type=F32)
-        outgoing[:, c] = rows.reshape(nv, 8, POINTS)
-
-    pl.semaphore_wait(barrier, nv - 1)
-    copies = []
-    for step in range(1, nv):
-        peer = (me + step) % nv
-        copy = pltpu.make_async_remote_copy(
-            src_ref=outgoing.at[peer],
-            dst_ref=arrived.at[me],
-            send_sem=send_sem.at[step - 1],
-            recv_sem=recv_sem.at[step - 1],
-            device_id={"valve": peer},
-            device_id_type=MESH,
-        )
-        copy.start()
-        copies.append(copy)
-    arrived[me] = outgoing[me]
-    for copy in copies:
-        copy.wait_recv()
-    for source in range(nv):
-        for c in range(5):
-            out_ref[c, source * CAPACITY : (source + 1) * CAPACITY, :] = arrived[source, c, 0:CAPACITY, :]
-    for copy in copies:
-        copy.wait_send()
-
-
-def fringe(nv, count, owner, update, index, weight):
-    blocks = index.shape[0]
-    smem = pl.BlockSpec(memory_space=pltpu.SMEM)
-    vmem = pl.BlockSpec(memory_space=VMEM)
-    return pl.pallas_call(
-        functools.partial(fringe_kernel, nv),
-        out_shape=jax.ShapeDtypeStruct((5, nv * CAPACITY, POINTS), F32),
-        in_specs=[smem, smem, vmem, vmem, vmem, vmem],
-        out_specs=vmem,
-        scratch_shapes=[
-            VMEM((5, PLANES, 8, CELLS), F32),
-            VMEM((5, blocks, POINTS), F32),
-            VMEM((nv, 5, 8, POINTS), F32),
-            VMEM((nv, 5, 8, POINTS), F32),
-            pltpu.SemaphoreType.DMA((nv - 1,)),
-            pltpu.SemaphoreType.DMA((nv - 1,)),
-        ],
-        compiler_params=pltpu.CompilerParams(collective_id=1, has_side_effects=True),
-    )(count, owner, owner, update, index, weight)
+    )(rhs, diag, lower, upper, index, weight, count, owner)
 
 
 def solution(mesh):
@@ -377,8 +462,7 @@
     nv = mesh.shape["valve"]
 
     def body(rhs, diag, lower, upper, index, weight, count, owner):
-        update = sweeps(nx, rhs, diag, lower, upper)
-        rows = fringe(nv, count, owner, update, index[0], weight[0])
+        update, rows = whole(nx, nv, rhs, diag, lower, upper, index[0], weight[0], count, owner)
         return update, jnp.transpose(rows, (1, 0, 2))[None]
 
     in_specs = (

time: 52 us -> 47.5 us (0.913)
  Pallas kernels: 48.8 us -> 43.7 us
  local copies, waits for them, and re-layouts: 2.24 us -> 2.96 us
    pallas_call x2 -> x1, Pallas kernels: 48.8 us -> 43.7 us  [whole(): pl.pallas_call(functools.partial(whole_kernel, nx, nv), out_shape=(jax.Sh...]
    unnamed x4 -> x2, local copies, waits for them, and re-layouts: 2.24 us -> 2.96 us
where the time goes in v2:
time: 47.5 us; the launch traced here: 47.3 us
  Pallas kernels  43.7 us (92%)
  local copies, waits for them, and re-layouts  2.96 us (6%)
  between operations  0.64 us (1%)
    pallas_call x1, Pallas kernels, whole(): pl.pallas_call(functools.partial(whole_kernel, nx, nv), out_shape=(jax.Sh...  43.7 us
    unnamed x2, local copies, waits for them, and re-layouts  2.96 us

profile of v2, /device:TPU:1, one launch (start us, length us, event | category | flops | bytes accessed | tf_op | source)
XLA Modules:
  0.0 47.3 jit_solution(8240491760324984303)
XLA Ops:
  0.6 43.7 %shard_map.95 = (f32[5,8,128]{2,1,0:T(8,128)}, f32[5,80,128]{2,1,0:T(8,128)}) custom-call(f32[5,8,128]{2,1,0:T(8,128)} %rhs_hbm.1, f32[5,5,8,128]{3,2,1,0:T(8,128)} %diag_hbm.1, f32[5,5,8,128]{3,2,1,0:T(8,128)} %lower_hbm.1, f32[5,5,8,128]{3,2,1,0:T(8,128)} %upper_hbm.1, s32[16,8,128]{2,1,0:T(8,128)} %bitcast.6, f32[16,8,128]{2,1,0:T(8,128)} %bitcast.7, ...), custom_call_target="tpu_custom_call" | custom-call | tf_op jit(solution)/shard_map/pallas_call | solution.py:407
  44.4 1.3 %copy.12 = f32[5,8,128]{2,1,0:T(8,128)} copy(f32[5,8,128]{2,1,0:T(8,128)} %get-tuple-element.8) | data formatting | bytes 40960
  45.7 1.6 %copy.13 = f32[1,80,5,128]{3,1,2,0:T(8,128)} copy(f32[1,80,5,128]{3,1,2,0:T(8,128)} %bitcast.5) | data formatting | bytes 409600

commit v3 on v2

--- a/solution.py
+++ b/solution.py
@@ -221,7 +221,6 @@
     up_matrices = backward_matrices(-compose(diag, upper_ref[...]), plane_levels)
     put(up_out, 0, up_matrices.reshape(25, PLANES, CELLS), 0)
     place(up_all, my_y, ROWS)[...] = up_out[...]
-    up_y = send_y(1, up_out, up_all, ROWS)
 
     for load in loads[4:]:
         load.wait()
@@ -251,6 +250,7 @@
         weight_ref[block] = jnp.where(lane < count_ref[0, block], weight_ref[block], 0.0)
 
     arrive(low_y)
+    up_y = send_y(1, up_out, up_all, ROWS)
     row_matrices, row_offsets = forward_scan(
         gathered(low_all, 0, 25, ROWS).reshape(5, 5, 8, CELLS), gathered(low_all, 25, 5, ROWS)
     )
@@ -407,8 +407,8 @@
     return pl.pallas_call(
         functools.partial(whole_kernel, nx, nv),
         out_shape=(
-            jax.ShapeDtypeStruct((5, PLANES, CELLS), F32),
-            jax.ShapeDtypeStruct((5, nv * CAPACITY, POINTS), F32),
+            VMEM((5, PLANES, CELLS), F32),
+            VMEM((5, nv * CAPACITY, POINTS), F32),
         ),
         in_specs=[hbm] * 8,
         out_specs=(vmem, vmem),

time: 47.5 us -> 46.9 us (0.987)
  local copies, waits for them, and re-layouts: 2.96 us -> 1.29 us
  Pallas kernels: 43.7 us -> 44.9 us
    unnamed x2, local copies, waits for them, and re-layouts: 2.96 us -> 1.29 us
    pallas_call x1, Pallas kernels: 43.7 us -> 44.9 us  [whole(): pl.pallas_call(functools.partial(whole_kernel, nx, nv), out_shape=(VMEM((...]
where the time goes in v3:
time: 46.9 us; the launch traced here: 46.8 us
  Pallas kernels  44.9 us (96%)
  local copies, waits for them, and re-layouts  1.29 us (3%)
  between operations  0.64 us (1%)
    pallas_call x1, Pallas kernels, whole(): pl.pallas_call(functools.partial(whole_kernel, nx, nv), out_shape=(VMEM((...  44.9 us
    unnamed x2, local copies, waits for them, and re-layouts  1.29 us

profile of v3, /device:TPU:1, one launch (start us, length us, event | category | flops | bytes accessed | tf_op | source)
XLA Modules:
  0.0 46.8 jit_solution(16112109244157317903)
XLA Ops:
  0.6 44.9 %shard_map.95 = (f32[5,8,128]{2,1,0:T(8,128)S(1)}, f32[5,80,128]{2,1,0:T(8,128)S(1)}) custom-call(f32[5,8,128]{2,1,0:T(8,128)} %rhs_hbm.1, f32[5,5,8,128]{3,2,1,0:T(8,128)} %diag_hbm.1, f32[5,5,8,128]{3,2,1,0:T(8,128)} %lower_hbm.1, f32[5,5,8,128]{3,2,1,0:T(8,128)} %upper_hbm.1, s32[16,8,128]{2,1,0:T(8,128)} %bitcast.6, f32[16,8,128]{2,1,0:T(8,128)} %bitcast.7, ...), custom_call_target="tpu_custom_call" | custom-call | tf_op jit(solution)/shard_map/pallas_call | solution.py:407
  45.5 0.6 %copy.12 = f32[5,8,128]{2,1,0:T(8,128)} copy(f32[5,8,128]{2,1,0:T(8,128)S(1)} %get-tuple-element.6) | data formatting | bytes 40960
  46.1 0.7 %copy.13 = f32[1,80,5,128]{3,1,2,0:T(8,128)} copy(f32[1,80,5,128]{3,1,2,0:T(8,128)S(1)} %bitcast.5) | data formatting | bytes 409600

commit v4 on v3

--- a/solution.py
+++ b/solution.py
@@ -258,13 +258,7 @@
     put(low_total, 25, row_offsets, 7)
     low_x = send_x(0, low_total, low_rows, ROWS)
 
-    arrive(up_y)
-    row_up = backward_matrices(gathered(up_all, 0, 25, ROWS).reshape(5, 5, 8, CELLS), row_levels)
-    put(up_total, 0, row_up.reshape(25, 8, CELLS), 0)
-    up_x = send_x(1, up_total, up_rows, ROWS)
-
     place(low_rows, my_x, ROWS)[...] = low_total[...]
-    place(up_rows, my_x, ROWS)[...] = up_total[...]
 
     def chain(rows, offsets_of, order, passes):
         state = [jnp.zeros((1, CELLS), F32) for _ in range(5)]
@@ -296,12 +290,19 @@
     put(off_out, 0, partial, 0)
     off_y = send_y(2, off_out, off_all, 8)
     place(off_all, my_y, 8)[...] = off_out[...]
-    arrive(up_x)
+
+    arrive(up_y)
+    row_up = backward_matrices(gathered(up_all, 0, 25, ROWS).reshape(5, 5, 8, CELLS), row_levels)
+    put(up_total, 0, row_up.reshape(25, 8, CELLS), 0)
+    up_x = send_x(1, up_total, up_rows, ROWS)
+    place(up_rows, my_x, ROWS)[...] = up_total[...]
+
     arrive(off_y)
     row_partial = backward_offsets(row_levels, gathered(off_all, 0, 5, 8))
     put(off_total, 0, row_partial, 0)
     off_x = send_x(2, off_total, off_rows, 8)
     place(off_rows, my_x, 8)[...] = off_total[...]
+    arrive(up_x)
     arrive(off_x)
     entering = chain(
         up_rows,

time: 46.9 us -> 44.7 us (0.953)
  Pallas kernels: 44.9 us -> 42.6 us
    pallas_call x1, Pallas kernels: 44.9 us -> 42.6 us  [whole(): pl.pallas_call(functools.partial(whole_kernel, nx, nv), out_shape=(VMEM((...]
where the time goes in v4:
time: 44.7 us; the launch traced here: 44.6 us
  Pallas kernels  42.6 us (95%)
  local copies, waits for them, and re-layouts  1.29 us (3%)
  between operations  0.64 us (1%)
    pallas_call x1, Pallas kernels, whole(): pl.pallas_call(functools.partial(whole_kernel, nx, nv), out_shape=(VMEM((...  42.6 us
    unnamed x2, local copies, waits for them, and re-layouts  1.29 us

profile of v4, /device:TPU:1, one launch (start us, length us, event | category | flops | bytes accessed | tf_op | source)
XLA Modules:
  0.0 44.6 jit_solution(9078992341873917251)
XLA Ops:
  0.6 42.6 %shard_map.95 = (f32[5,8,128]{2,1,0:T(8,128)S(1)}, f32[5,80,128]{2,1,0:T(8,128)S(1)}) custom-call(f32[5,8,128]{2,1,0:T(8,128)} %rhs_hbm.1, f32[5,5,8,128]{3,2,1,0:T(8,128)} %diag_hbm.1, f32[5,5,8,128]{3,2,1,0:T(8,128)} %lower_hbm.1, f32[5,5,8,128]{3,2,1,0:T(8,128)} %upper_hbm.1, s32[16,8,128]{2,1,0:T(8,128)} %bitcast.6, f32[16,8,128]{2,1,0:T(8,128)} %bitcast.7, ...), custom_call_target="tpu_custom_call" | custom-call | tf_op jit(solution)/shard_map/pallas_call | solution.py:408
  43.3 0.6 %copy.12 = f32[5,8,128]{2,1,0:T(8,128)} copy(f32[5,8,128]{2,1,0:T(8,128)S(1)} %get-tuple-element.6) | data formatting | bytes 40960
  43.9 0.7 %copy.13 = f32[1,80,5,128]{3,1,2,0:T(8,128)} copy(f32[1,80,5,128]{3,1,2,0:T(8,128)S(1)} %bitcast.5) | data formatting | bytes 409600

commit v5 on v4

--- a/solution.py
+++ b/solution.py
@@ -155,13 +155,13 @@
         return {"bulk": ((my_x + step) % nx) * NY + my_y}
 
     barrier = pltpu.get_barrier_semaphore()
-    for step in range(1, NY):
-        pl.semaphore_signal(barrier, inc=1, device_id=y_peer(step), device_id_type=MESH)
+    for step in sorted(range(1, nv), key=lambda step: -min(step, nv - step)):
+        pl.semaphore_signal(barrier, inc=1, device_id={"valve": (me + step) % nv}, device_id_type=MESH)
+        if step < NY:
+            near = (4, 3, 5, 2, 6, 1, 7)[NY - 1 - step]
+            pl.semaphore_signal(barrier, inc=1, device_id=y_peer(near), device_id_type=MESH)
     for step in range(1, nx):
         pl.semaphore_signal(barrier, inc=1, device_id=x_peer(step), device_id_type=MESH)
-
-    for step in range(1, nv):
-        pl.semaphore_signal(barrier, inc=1, device_id={"valve": (me + step) % nv}, device_id_type=MESH)
 
     def place(ref, index, rows):
         return ref.at[pl.ds(pl.multiple_of(index * rows, 8), rows), :]
@@ -249,8 +249,10 @@
     for block in range(blocks):
         weight_ref[block] = jnp.where(lane < count_ref[0, block], weight_ref[block], 0.0)
 
+    for copy in low_y:
+        copy.wait_send()
+    up_y = send_y(1, up_out, up_all, ROWS)
     arrive(low_y)
-    up_y = send_y(1, up_out, up_all, ROWS)
     row_matrices, row_offsets = forward_scan(
         gathered(low_all, 0, 25, ROWS).reshape(5, 5, 8, CELLS), gathered(low_all, 25, 5, ROWS)
     )
@@ -397,7 +399,7 @@
                 fringe_ref[c, base + slot : base + slot + count, :] = arrived[number // 8, source, row : row + count, :]
                 slot += count
 
-    for copies in (low_y, up_y, low_x, up_x, off_y, off_x, sent):
+    for copies in (up_y, low_x, up_x, off_y, off_x, sent):
         for copy in copies:
             copy.wait_send()
 

time: 44.7 us -> 44.9 us (level)
  no operation moved by 1% of the time
where the time goes in v5:
time: 44.9 us; the launch traced here: 44.8 us
  Pallas kernels  42.8 us (95%)
  local copies, waits for them, and re-layouts  1.29 us (3%)
  between operations  0.64 us (1%)
    pallas_call x1, Pallas kernels, whole(): pl.pallas_call(functools.partial(whole_kernel, nx, nv), out_shape=(VMEM((...  42.8 us
    unnamed x2, local copies, waits for them, and re-layouts  1.29 us

profile of v5, /device:TPU:1, one launch (start us, length us, event | category | flops | bytes accessed | tf_op | source)
XLA Modules:
  0.0 44.8 jit_solution(3070911694297062643)
XLA Ops:
  0.6 42.8 %shard_map.95 = (f32[5,8,128]{2,1,0:T(8,128)S(1)}, f32[5,80,128]{2,1,0:T(8,128)S(1)}) custom-call(f32[5,8,128]{2,1,0:T(8,128)} %rhs_hbm.1, f32[5,5,8,128]{3,2,1,0:T(8,128)} %diag_hbm.1, f32[5,5,8,128]{3,2,1,0:T(8,128)} %lower_hbm.1, f32[5,5,8,128]{3,2,1,0:T(8,128)} %upper_hbm.1, s32[16,8,128]{2,1,0:T(8,128)} %bitcast.6, f32[16,8,128]{2,1,0:T(8,128)} %bitcast.7, ...), custom_call_target="tpu_custom_call" | custom-call | tf_op jit(solution)/shard_map/pallas_call | solution.py:410
  43.5 0.6 %copy.12 = f32[5,8,128]{2,1,0:T(8,128)} copy(f32[5,8,128]{2,1,0:T(8,128)S(1)} %get-tuple-element.6) | data formatting | bytes 40960
  44.1 0.7 %copy.13 = f32[1,80,5,128]{3,1,2,0:T(8,128)} copy(f32[1,80,5,128]{3,1,2,0:T(8,128)S(1)} %bitcast.5) | data formatting | bytes 409600

commit v6 on v5

--- a/solution.py
+++ b/solution.py
@@ -335,18 +335,18 @@
                 products[c, pl.ds(pl.multiple_of(block * 8, 8), 8), :] = weights * picked
             return carry
 
-        lax.fori_loop(0, blocks, step, 0, unroll=2)
+        lax.fori_loop(0, blocks, step, 0, unroll=8)
 
     def selected(selection, first, last):
         total = None
         for c in range(first, last):
-            part = jnp.dot(
-                selection[:, (c - first) * CELLS : (c - first + 1) * CELLS],
-                products[c],
-                precision=lax.Precision.HIGHEST,
-                preferred_element_type=F32,
-            )
-            total = part if total is None else total + part
+            chosen = selection[:, (c - first) * CELLS : (c - first + 1) * CELLS].astype(jnp.bfloat16)
+            rest = products[c]
+            for _ in range(3):
+                piece = rest.astype(jnp.bfloat16)
+                rest = rest - piece.astype(F32)
+                part = jnp.dot(chosen, piece, preferred_element_type=F32)
+                total = part if total is None else total + part
         return total
 
     def send_v(stage, source_of, target_of):

time: 44.9 us -> 43.3 us (0.964)
  Pallas kernels: 42.8 us -> 41.2 us
    pallas_call x1, Pallas kernels: 42.8 us -> 41.2 us  [whole(): pl.pallas_call(functools.partial(whole_kernel, nx, nv), out_shape=(VMEM((...]
where the time goes in v6:
time: 43.3 us; the launch traced here: 43.1 us
  Pallas kernels  41.2 us (95%)
  local copies, waits for them, and re-layouts  1.29 us (3%)
  between operations  0.64 us (1%)
    pallas_call x1, Pallas kernels, whole(): pl.pallas_call(functools.partial(whole_kernel, nx, nv), out_shape=(VMEM((...  41.2 us
    unnamed x2, local copies, waits for them, and re-layouts  1.29 us

profile of v6, /device:TPU:1, one launch (start us, length us, event | category | flops | bytes accessed | tf_op | source)
XLA Modules:
  0.0 43.1 jit_solution(7133718717700817425)
XLA Ops:
  0.6 41.2 %shard_map.95 = (f32[5,8,128]{2,1,0:T(8,128)S(1)}, f32[5,80,128]{2,1,0:T(8,128)S(1)}) custom-call(f32[5,8,128]{2,1,0:T(8,128)} %rhs_hbm.1, f32[5,5,8,128]{3,2,1,0:T(8,128)} %diag_hbm.1, f32[5,5,8,128]{3,2,1,0:T(8,128)} %lower_hbm.1, f32[5,5,8,128]{3,2,1,0:T(8,128)} %upper_hbm.1, s32[16,8,128]{2,1,0:T(8,128)} %bitcast.6, f32[16,8,128]{2,1,0:T(8,128)} %bitcast.7, ...), custom_call_target="tpu_custom_call" | custom-call | tf_op jit(solution)/shard_map/pallas_call | solution.py:410
  41.8 0.6 %copy.12 = f32[5,8,128]{2,1,0:T(8,128)} copy(f32[5,8,128]{2,1,0:T(8,128)S(1)} %get-tuple-element.6) | data formatting | bytes 40960
  42.5 0.7 %copy.13 = f32[1,80,5,128]{3,1,2,0:T(8,128)} copy(f32[1,80,5,128]{3,1,2,0:T(8,128)S(1)} %bitcast.5) | data formatting | bytes 409600
